TPU v7x, 32 devices: a whole 2x2x4 slice. The times are simulated.
32 devices in a mesh: gx: 16 (over z, y, core), gy: 2 (over x).
Axes of the slice: x: 2, y: 2, z: 4, core: 2. Of those that a mesh axis runs over, the one named last changes fastest.
Arguments:
- positions: float32 [3, 65536], P(None, ('gx', 'gy')), may hold values from 0 to 6
- features: bfloat16 [64, 65536], P(None, ('gx', 'gy')), may hold values from -6 to 6
- halo_lists: int32 [2, 49152], P(None, ('gx', 'gy')), may hold values from 0 to 2047
- local_pairs: int32 [4, 196608], P(None, ('gx', 'gy')), may hold values from 0 to 2047, as said below
- cross_x: int32 [4, 65536], P(None, ('gx', 'gy')), may hold values from 0 to 2047, as said below
- cross_y: int32 [4, 65536], P(None, ('gx', 'gy')), may hold values from 0 to 2047, as said below
- pair_counts: int32 [32, 3], P(('gx', 'gy')), may hold values from 256 to 6144, as said below
- w_rbf: bfloat16 [8, 256], replicated, may hold values from -2 to 2
- w_src: bfloat16 [64, 256], replicated, may hold values from -0.75 to 0.75
- w_dst: bfloat16 [64, 256], replicated, may hold values from -0.75 to 0.75
- species_src: bfloat16 [4, 256], replicated, may hold values from -3 to 3
- species_dst: bfloat16 [4, 256], replicated, may hold values from -3 to 3
- w_hidden: bfloat16 [256, 256], replicated, may hold values from -0.375 to 0.375
- w_latent: bfloat16 [256, 64], replicated, may hold values from -0.375 to 0.375
- w_energy: float32 [64], replicated, may hold values from -0.75 to 0.75
Outputs:
- energy: float32 [1], replicated
- forces: float32 [3, 65536], P(None, ('gx', 'gy'))
- feature_grads: float32 [64, 65536], P(None, ('gx', 'gy'))
Inputs may be any that keep to these rules, and one draw needn't show every extreme that they name: `local_pairs`: rows 0 and 1 are different atoms of the block, below 2048; rows 2 and 3 are species below 4. `cross_x`: row 0 an atom below 2048, row 1 a slot below 1536, rows 2 and 3 species below 4. `cross_y`: row 0 an atom below 2048, row 1 a slot below 1536, rows 2 and 3 species below 4. `pair_counts`: column 0 counts live slots of local_pairs (at most 6144), columns 1 and 2 those of cross_x and cross_y (at most 2048); live slots come first; some device is full in each column.
All inputs are finite; a program needn't handle non-finite values.
Results may differ from a plain program's by a relative error of at most 0.0095.
Values may be sent and summed in bfloat16 or wider, within the bound.
No kernel may reach another device: no remote copies, remote signals or barrier semaphores. Data moves between devices by JAX's collectives and lax.ppermute only.
A program may use at most 64 MiB of HBM per device.

v0:
```python
import jax
import jax.numpy as jnp
from jax import lax
from jax.sharding import PartitionSpec as P

BLOCK = 512


cutoff_radius = 6.0
block_edge = 6.0
softening = 0.1


def shifted(array, axis, by):
    length = lax.axis_size(axis)
    return lax.ppermute(array, axis, [(i, (i + by) % length) for i in range(length)])


def pair_energy(
    src_pos, src_feat, dst_pos, dst_feat, spec_src, spec_dst, live_mask, offset, weights
):
    w_rbf, w_src, w_dst, species_src, species_dst, w_hidden, w_latent, w_energy = weights
    displace = dst_pos + offset[:, None] - src_pos
    radius = jnp.sqrt(jnp.sum(displace * displace, axis=0) + softening)
    orders = jnp.arange(1, w_rbf.shape[0] + 1).astype(jnp.float32)[:, None]
    basis = (jnp.sin(orders * (jnp.pi / cutoff_radius) * radius[None, :]) / radius[None, :]).astype(
        jnp.bfloat16
    )
    kinds = jnp.arange(species_src.shape[0], dtype=jnp.int32)[:, None]
    onehot_src = (spec_src[None, :] == kinds).astype(jnp.bfloat16)
    onehot_dst = (spec_dst[None, :] == kinds).astype(jnp.bfloat16)
    pre = jnp.dot(w_rbf.T, basis, preferred_element_type=jnp.float32)
    pre = pre + jnp.dot(w_src.T, src_feat.astype(jnp.bfloat16), preferred_element_type=jnp.float32)
    pre = pre + jnp.dot(w_dst.T, dst_feat.astype(jnp.bfloat16), preferred_element_type=jnp.float32)
    pre = pre + jnp.dot(species_src.T, onehot_src, preferred_element_type=jnp.float32)
    pre = pre + jnp.dot(species_dst.T, onehot_dst, preferred_element_type=jnp.float32)
    hidden = jax.nn.silu(pre).astype(jnp.bfloat16)
    second = jax.nn.silu(jnp.dot(w_hidden.T, hidden, preferred_element_type=jnp.float32)).astype(
        jnp.bfloat16
    )
    latent = jnp.dot(w_latent.T, second, preferred_element_type=jnp.float32)
    ratio = jnp.minimum(radius / cutoff_radius, 1.0)
    envelope = (1.0 - ratio**2) ** 2
    scores = jnp.dot(w_energy, latent, precision=lax.Precision.HIGHEST)
    return jnp.sum(envelope * scores * live_mask)


def block_grads(
    src_pos, src_feat, dst_pos, dst_feat, spec_src, spec_dst, live_mask, offset, weights
):

    def energy_of(pos_one, feat_one, pos_two, feat_two):
        return pair_energy(
            pos_one, feat_one, pos_two, feat_two, spec_src, spec_dst, live_mask, offset, weights
        )

    energy, pullback = jax.vjp(
        energy_of, src_pos, src_feat.astype(jnp.float32), dst_pos, dst_feat.astype(jnp.float32)
    )
    return (energy, pullback(jnp.ones_like(energy)))


def run_edges(
    src_pos, src_feat, dst_pos, dst_feat, spec_src, spec_dst, live_mask, live_count, offset, weights
):
    inputs = (src_pos, src_feat, dst_pos, dst_feat, spec_src, spec_dst, live_mask)
    edges = src_pos.shape[1]
    filled = (live_count + BLOCK - 1) // BLOCK
    start_grads = (
        jnp.zeros((3, edges), jnp.float32),
        jnp.zeros((src_feat.shape[0], edges), jnp.float32),
        jnp.zeros((3, edges), jnp.float32),
        jnp.zeros((dst_feat.shape[0], edges), jnp.float32),
    )

    def visit_live(index, carry):
        total, grads = carry
        begin = index * BLOCK
        blocks = tuple(
            (lax.dynamic_slice_in_dim(item, begin, BLOCK, axis=item.ndim - 1) for item in inputs)
        )
        energy, parts = block_grads(*blocks, offset, weights)
        grads = tuple(
            (
                lax.dynamic_update_slice_in_dim(whole, piece, begin, axis=1)
                for whole, piece in zip(grads, parts)
            )
        )
        return (total + energy, grads)

    return lax.fori_loop(0, filled, visit_live, (jnp.zeros((), jnp.float32), start_grads))


def on_device(
    positions,
    features,
    halo_lists,
    local_pairs,
    cross_x,
    cross_y,
    pair_counts,
    w_rbf,
    w_src,
    w_dst,
    species_src,
    species_dst,
    w_hidden,
    w_latent,
    w_energy,
):
    weights = (w_rbf, w_src, w_dst, species_src, species_dst, w_hidden, w_latent, w_energy)
    atoms = positions.shape[1]
    halo_size = halo_lists.shape[1]
    width = features.shape[0]
    list_x = halo_lists[0]
    list_y = halo_lists[1]
    got_pos_x = shifted(positions[:, list_x], "gx", -1)
    got_feat_x = shifted(features[:, list_x], "gx", -1)
    got_pos_y = shifted(positions[:, list_y], "gy", -1)
    got_feat_y = shifted(features[:, list_y], "gy", -1)
    zero_off = jnp.zeros((3,), jnp.float32)
    off_x = jnp.array([block_edge, 0.0, 0.0], jnp.float32)
    off_y = jnp.array([0.0, block_edge, 0.0], jnp.float32)
    counts = pair_counts[0]
    slots_loc = jnp.arange(local_pairs.shape[1], dtype=jnp.int32)
    slots_cross = jnp.arange(cross_x.shape[1], dtype=jnp.int32)
    live_loc = (slots_loc < counts[0]).astype(jnp.float32)
    flag_x = (slots_cross < counts[1]).astype(jnp.int32)
    flag_y = (slots_cross < counts[2]).astype(jnp.int32)
    source, target = (local_pairs[0], local_pairs[1])
    energy_loc, grads = run_edges(
        positions[:, source],
        features[:, source],
        positions[:, target],
        features[:, target],
        local_pairs[2],
        local_pairs[3],
        live_loc,
        counts[0],
        zero_off,
        weights,
    )
    grad_pos = (
        jnp.zeros((3, atoms), jnp.float32).at[:, source].add(grads[0]).at[:, target].add(grads[2])
    )
    grad_feat = (
        jnp.zeros((width, atoms), jnp.float32)
        .at[:, source]
        .add(grads[1])
        .at[:, target]
        .add(grads[3])
    )
    source_x, slot_x = (cross_x[0], cross_x[1])
    src_pos_x = positions[:, source_x]
    src_feat_x = features[:, source_x]
    energy_x, grads_x = run_edges(
        src_pos_x,
        src_feat_x,
        got_pos_x[:, slot_x],
        got_feat_x[:, slot_x],
        cross_x[2],
        cross_x[3],
        flag_x.astype(jnp.float32),
        counts[1],
        off_x,
        weights,
    )
    grad_pos = grad_pos.at[:, source_x].add(grads_x[0])
    grad_feat = grad_feat.at[:, source_x].add(grads_x[1])
    source_y, slot_y = (cross_y[0], cross_y[1])
    src_pos_y = positions[:, source_y]
    src_feat_y = features[:, source_y]
    energy_y, grads_y = run_edges(
        src_pos_y,
        src_feat_y,
        got_pos_y[:, slot_y],
        got_feat_y[:, slot_y],
        cross_y[2],
        cross_y[3],
        flag_y.astype(jnp.float32),
        counts[2],
        off_y,
        weights,
    )
    grad_pos = grad_pos.at[:, source_y].add(grads_y[0])
    grad_feat = grad_feat.at[:, source_y].add(grads_y[1])
    lent_pos_x = jnp.zeros((3, halo_size), jnp.float32).at[:, slot_x].add(grads_x[2])
    lent_feat_x = jnp.zeros((width, halo_size), jnp.float32).at[:, slot_x].add(grads_x[3])
    back_pos_x, back_feat_x = shifted((lent_pos_x, lent_feat_x), "gx", 1)
    lent_pos_y = jnp.zeros((3, halo_size), jnp.float32).at[:, slot_y].add(grads_y[2])
    lent_feat_y = jnp.zeros((width, halo_size), jnp.float32).at[:, slot_y].add(grads_y[3])
    back_pos_y, back_feat_y = shifted((lent_pos_y, lent_feat_y), "gy", 1)
    grad_pos = grad_pos.at[:, list_x].add(back_pos_x).at[:, list_y].add(back_pos_y)
    grad_feat = grad_feat.at[:, list_x].add(back_feat_x).at[:, list_y].add(back_feat_y)
    total = lax.psum(energy_loc + energy_x + energy_y, ("gx", "gy"))
    atoms_all = atoms * lax.axis_size("gx") * lax.axis_size("gy")
    energy = (total / atoms_all).reshape(1)
    return (energy, -grad_pos, grad_feat)


def solution(mesh):
    return jax.shard_map(
        on_device,
        mesh=mesh,
        in_specs=(
            P(None, ("gx", "gy")),
            P(None, ("gx", "gy")),
            P(None, ("gx", "gy")),
            P(None, ("gx", "gy")),
            P(None, ("gx", "gy")),
            P(None, ("gx", "gy")),
            P(("gx", "gy"), None),
            P(),
            P(),
            P(),
            P(),
            P(),
            P(),
            P(),
            P(),
        ),
        out_specs=(P(), P(None, ("gx", "gy")), P(None, ("gx", "gy"))),
        check_vma=False,
    )
```

profile of v0, /device:TPU:0, one launch (start us, length us, event | category | flops | bytes accessed | tf_op | source)
XLA Modules:
  0.0 768.6 jit_solution(1176307451014661208)
XLA Ops:
  31.0 20.9 %gather_fusion.1 = f32[6144,3]{1,0:T(8,128)} fusion(f32[3,2048]{0,1:T(8,128)S(1)} %copy.112, s32[6144]{0:T(1024)S(1)} %broadcast_clamp_fusion), kind=kCustom, calls=%fused_computation.1 | custom fusion | bytes 172032 | tf_op jit(solution)/shard_map/gather | solution.py:132
  51.9 22.1 %gather_fusion.2 = bf16[6144,64]{1,0:T(8,128)(2,1)} fusion(bf16[64,2048]{0,1:T(8,128)(2,1)S(1)} %copy.114, s32[6144]{0:T(1024)S(1)} %broadcast_clamp_fusion), kind=kCustom, calls=%fused_computation.2 | custom fusion | bytes 1597440 | tf_op jit(solution)/shard_map/gather | solution.py:133
  74.0 20.9 %gather_fusion = f32[6144,3]{1,0:T(8,128)} fusion(f32[3,2048]{0,1:T(8,128)S(1)} %copy.112, s32[6144]{0:T(1024)S(1)} %broadcast_clamp_fusion.1), kind=kCustom, calls=%fused_computation | custom fusion | bytes 172032 | tf_op jit(solution)/shard_map/gather | solution.py:134
  94.9 22.0 %gather_fusion.3 = bf16[6144,64]{1,0:T(8,128)(2,1)} fusion(bf16[64,2048]{0,1:T(8,128)(2,1)S(1)} %copy.114, s32[6144]{0:T(1024)S(1)} %broadcast_clamp_fusion.1), kind=kCustom, calls=%fused_computation.3 | custom fusion | bytes 1597440 | tf_op jit(solution)/shard_map/gather | solution.py:135
  117.6 7.6 gather_fusion.6
  125.2 6.2 gather_fusion.7
  132.0 7.6 gather_fusion.12
  139.6 8.0 %gather_fusion.13 = bf16[2048,64]{1,0:T(8,128)(2,1)} fusion(bf16[64,2048]{0,1:T(8,128)(2,1)S(1)} %copy.114, s32[2048]{0:T(1024)S(1)} %broadcast_clamp_fusion.4), kind=kCustom, calls=%fused_computation.13 | custom fusion | bytes 532480 | tf_op jit(solution)/shard_map/gather | solution.py:172
  160.3 7.6 gather_fusion.5
  169.8 7.6 gather_fusion.11
  179.0 6.2 gather_fusion.9
  185.6 17.9 %while.57 = (s32[]{:T(128)}, f32[]{:T(128)}, f32[3,2048]{1,0:T(4,128)S(1)}, f32[64,2048]{1,0:T(8,128)S(1)}, f32[3,2048]{1,0:T(4,128)S(1)}, /*index=5*/f32[64,204...) while((s32[]{:T(128)}, f32[]{:T(128)}, ...), condition=%wide.region_11.12_spmd.clone, body=%wide.region_6.11_spmd.sunk.clone.sunk | while | flops 246594080 | bytes 9612223 | solution.py:91
  203.5 6.2 gather_fusion.15
  210.1 41.6 %while.58 = (s32[]{:T(128)}, f32[]{:T(128)}, f32[3,2048]{1,0:T(4,128)S(1)}, f32[64,2048]{1,0:T(8,128)S(1)}, f32[3,2048]{1,0:T(4,128)S(1)}, /*index=5*/f32[64,204...) while((s32[]{:T(128)}, f32[]{:T(128)}, ...), condition=%wide.region_17.18_spmd.clone, body=%wide.region_12.17_spmd.sunk.clone.sunk | while | flops 246594080 | bytes 9743323 | solution.py:91
  253.1 12.0 %scatter_custom_fusion.12 = f32[64,1536]{0,1:T(8,128)S(1)} fusion(s32[2048]{0:T(1024)} %bitcast.415, f32[2048,64]{1,0:T(8,128)} %copy.162, f32[]{:T(128)} %constant.142.clone.1), kind=kCustom, calls=%fused_computation.275 | custom fusion | flops 131072 | bytes 393728 | tf_op jit(solution)/shard_map/scatter-add | solution.py:188
  266.5 11.8 %scatter_custom_fusion.14 = f32[64,1536]{0,1:T(8,128)S(1)} fusion(s32[2048]{0:T(1024)} %bitcast.412, f32[2048,64]{1,0:T(8,128)S(1)} %copy.165, f32[]{:T(128)} %constant.142.clone.1), kind=kCustom, calls=%fused_computation.273 | custom fusion | flops 131072 | bytes 393728 | tf_op jit(solution)/shard_map/scatter-add | solution.py:191
  279.7 11.8 %scatter_custom_fusion.4 = f32[3,1536]{0,1:T(8,128)S(1)} fusion(s32[2048]{0:T(1024)} %bitcast.416, f32[2048,3]{1,0:T(8,128)S(1)} %copy.152, f32[]{:T(128)} %constant.142.clone.1), kind=kCustom, calls=%fused_computation.279 | custom fusion | flops 6144 | bytes 18944 | tf_op jit(solution)/shard_map/scatter-add | solution.py:187
  292.7 11.8 %scatter_custom_fusion.6 = f32[3,1536]{0,1:T(8,128)S(1)} fusion(s32[2048]{0:T(1024)} %bitcast.413, f32[2048,3]{1,0:T(8,128)S(1)} %copy.155, f32[]{:T(128)} %constant.142.clone.1), kind=kCustom, calls=%fused_computation.277 | custom fusion | flops 6144 | bytes 18944 | tf_op jit(solution)/shard_map/scatter-add | solution.py:190
  308.8 159.8 %while.56 = (s32[]{:T(128)}, f32[]{:T(128)}, f32[3,6144]{1,0:T(4,128)S(1)}, f32[64,6144]{1,0:T(8,128)S(1)}, f32[3,6144]{1,0:T(4,128)S(1)}, /*index=5*/f32[64,614...) while((s32[]{:T(128)}, f32[]{:T(128)}, ...), condition=%wide.region_5.6_spmd, body=%wide.region_0.5_spmd.sunk | while | flops 246594080 | bytes 9610155 | solution.py:91
  477.6 33.7 %scatter_custom_fusion.8 = f32[64,2048]{0,1:T(8,128)S(1)} fusion(s32[6144]{0:T(1024)} %bitcast.403, f32[6144,64]{1,0:T(8,128)} %copy.158, f32[]{:T(128)} %constant.142.clone.1), kind=kCustom, calls=%fused_computation.269 | custom fusion | flops 393216 | bytes 524800 | tf_op jit(solution)/shard_map/scatter-add | solution.py:149
  511.4 33.9 %scatter_fusion.5 = f32[64,2048]{0,1:T(8,128)S(1)} fusion(f32[64,2048]{0,1:T(8,128)S(1)} %scatter_custom_fusion.8, s32[6144]{0:T(1024)S(1)} %bitcast.387, f32[6144,64]{1,0:T(8,128)} %copy.159), kind=kCustom, calls=%fused_computation.25 | custom fusion | flops 393216 | bytes 4743168 | tf_op jit(solution)/shard_map/scatter-add | solution.py:151
  545.3 33.7 %scatter_custom_fusion = f32[3,2048]{0,1:T(8,128)S(1)} fusion(s32[6144]{0:T(1024)} %bitcast.404, f32[6144,3]{1,0:T(8,128)} %copy.148, f32[]{:T(128)} %constant.142.clone.1), kind=kCustom, calls=%fused_computation.271 | custom fusion | flops 18432 | bytes 25088 | tf_op jit(solution)/shard_map/scatter-add | solution.py:144
  579.0 33.9 %scatter_fusion = f32[3,2048]{0,1:T(8,128)S(1)} fusion(f32[3,2048]{0,1:T(8,128)S(1)} %scatter_custom_fusion, s32[6144]{0:T(1024)S(1)} %bitcast.388, f32[6144,3]{1,0:T(8,128)} %copy.149), kind=kCustom, calls=%fused_computation.17 | custom fusion | flops 18432 | bytes 245760 | tf_op jit(solution)/shard_map/scatter-add | solution.py:144
  612.9 53.5 %psum.7 = f32[]{:T(128)} all-reduce(f32[]{:T(128)S(6)} %add.371), channel_id=1, replica_groups=mesh['gx'=16,'gy'=2] {'gx','gy'}, use_global_device_ids=true, to_apply=%region_18.19 | all-reduce | flops 1 | bytes 8 | tf_op jit(solution)/shard_map/psum | solution.py:195
  672.9 11.9 %scatter_fusion.6 = f32[64,2048]{0,1:T(8,128)S(1)} fusion(f32[64,2048]{0,1:T(8,128)S(1)} %scatter_fusion.5, s32[2048]{0:T(1024)S(1)} %bitcast.393, f32[2048,64]{1,0:T(8,128)S(1)} %copy.160), kind=kCustom, calls=%fused_computation.26 | custom fusion | flops 131072 | bytes 1581056 | tf_op jit(solution)/shard_map/scatter-add | solution.py:169
  684.8 12.2 %scatter_fusion.7 = f32[64,2048]{0,1:T(8,128)S(1)} fusion(f32[64,2048]{0,1:T(8,128)S(1)} %scatter_fusion.6, s32[2048]{0:T(1024)S(1)} %bitcast.396, f32[2048,64]{1,0:T(8,128)} %copy.161), kind=kCustom, calls=%fused_computation.27 | custom fusion | flops 131072 | bytes 1581056 | tf_op jit(solution)/shard_map/scatter-add | solution.py:186
  697.0 12.2 %scatter_fusion.1 = f32[3,2048]{0,1:T(8,128)S(1)} fusion(f32[3,2048]{0,1:T(8,128)S(1)} %scatter_fusion, s32[2048]{0:T(1024)S(1)} %bitcast.394, f32[2048,3]{1,0:T(8,128)} %copy.150), kind=kCustom, calls=%fused_computation.18 | custom fusion | flops 6144 | bytes 81920 | tf_op jit(solution)/shard_map/scatter-add | solution.py:168
  709.3 12.2 %scatter_fusion.2 = f32[3,2048]{0,1:T(8,128)S(1)} fusion(f32[3,2048]{0,1:T(8,128)S(1)} %scatter_fusion.1, s32[2048]{0:T(1024)S(1)} %bitcast.397, f32[2048,3]{1,0:T(8,128)} %copy.151), kind=kCustom, calls=%fused_computation.19 | custom fusion | flops 6144 | bytes 81920 | tf_op jit(solution)/shard_map/scatter-add | solution.py:185
  725.1 9.1 %scatter_fusion.3 = f32[3,2048]{0,1:T(8,128)S(1)} fusion(f32[3,2048]{0,1:T(8,128)S(1)} %scatter_fusion.2, s32[1536]{0:T(1024)S(1)} %get-tuple-element.733, f32[1536,3]{1,0:T(8,128)S(1)} %copy.154), kind=kCustom, calls=%fused_computation.21 | custom fusion | flops 4608 | bytes 61440 | tf_op jit(solution)/shard_map/scatter-add | solution.py:193
  734.3 9.8 %scatter_fusion.4 = f32[3,2048]{0,1:T(8,128)S(1)} fusion(f32[3,2048]{0,1:T(8,128)S(1)} %scatter_fusion.3, s32[1536]{0:T(1024)S(1)} %get-tuple-element.732, f32[1536,3]{1,0:T(8,128)} %copy.157), kind=kCustom, calls=%fused_computation.23 | custom fusion | flops 4608 | bytes 61440 | tf_op jit(solution)/shard_map/scatter-add | solution.py:193
  747.6 9.1 %scatter_fusion.8 = f32[64,2048]{0,1:T(8,128)S(1)} fusion(f32[64,2048]{0,1:T(8,128)S(1)} %scatter_fusion.7, s32[1536]{0:T(1024)S(1)} %get-tuple-element.733, f32[1536,64]{1,0:T(8,128)S(1)} %copy.164), kind=kCustom, calls=%fused_computation.29 | custom fusion | flops 98304 | bytes 1185792 | tf_op jit(solution)/shard_map/scatter-add | solution.py:194
  756.8 9.1 %scatter_fusion.9 = f32[64,2048]{0,1:T(8,128)S(1)} fusion(f32[64,2048]{0,1:T(8,128)S(1)} %scatter_fusion.8, s32[1536]{0:T(1024)S(1)} %get-tuple-element.732, f32[1536,64]{1,0:T(8,128)S(1)} %copy.167), kind=kCustom, calls=%fused_computation.31 | custom fusion | flops 98304 | bytes 1185792 | tf_op jit(solution)/shard_map/scatter-add | solution.py:194
  (499 shorter events, 285.5 us)
Async XLA Ops:
  0.6 10.4 %copy-start.11 = (bf16[64,2048]{1,0:T(8,128)(2,1)S(1)}, bf16[64,2048]{1,0:T(8,128)(2,1)}, u32[]{:S(2)}) copy-start(bf16[64,2048]{1,0:T(8,128)(2,1)} %param.24) | copy-start | bytes 786436
  5.5 154.5 %collective-permute-start = (f32[3,1536]{1,0:T(4,128)S(1)}, f32[3,1536]{1,0:T(4,128)S(1)}, u32[]{:S(2)}, u32[]{:S(2)}) collective-permute-start(f32[3,1536]{1,0:T(4,128)S(1)} %copy.121), channel_id=1, source_target_pairs={{0,30},{2,0},{4,2},{6,4},{8,6},{10,8},{12,10},{14,12},{16,14},{18,... | collective-permute-start | bytes 55304 | tf_op jit(solution)/shard_map/ppermute | solution.py:16
  15.3 10.2 %copy-start.19 = (s32[4,6144]{1,0:T(4,128)S(1)}, s32[4,6144]{1,0:T(4,128)}, u32[]{:S(2)}) copy-start(s32[4,6144]{1,0:T(4,128)} %param.26) | copy-start | bytes 294916
  15.3 11.0 %copy-start.21 = (s32[4,2048]{1,0:T(4,128)S(1)}, s32[4,2048]{1,0:T(4,128)}, u32[]{:S(2)}) copy-start(s32[4,2048]{1,0:T(4,128)} %param.27) | copy-start | bytes 98308
  15.3 11.1 %copy-start.22 = (s32[4,2048]{1,0:T(4,128)S(1)}, s32[4,2048]{1,0:T(4,128)}, u32[]{:S(2)}) copy-start(s32[4,2048]{1,0:T(4,128)} %param.28) | copy-start | bytes 98308
  15.3 163.7 %collective-permute-start.1 = (bf16[64,1536]{0,1:T(8,128)(2,1)}, bf16[64,1536]{0,1:T(8,128)(2,1)S(1)}, u32[]{:S(2)}, u32[]{:S(2)}) collective-permute-start(bf16[64,1536]{0,1:T(8,128)(2,1)} %bitcast.32), channel_id=1, source_target_pairs={{0,30},{2,0},{4,2},{6,4},{8,6},{10,8},{12,10},{14,12},{16,14},{18,... | collective-permute-start | bytes 589832 | tf_op jit(solution)/shard_map/ppermute | solution.py:16
  16.1 11.0 %copy-start.26 = (s32[1,3]{1,0:T(1,128)S(1)}, s32[1,3]{1,0:T(1,128)}, u32[]{:S(2)}) copy-start(s32[1,3]{1,0:T(1,128)} %param.29) | copy-start | bytes 40
  19.5 149.9 %collective-permute-start.2 = (f32[3,1536]{1,0:T(4,128)}, f32[3,1536]{1,0:T(4,128)S(1)}, u32[]{:S(2)}, u32[]{:S(2)}) collective-permute-start(f32[3,1536]{1,0:T(4,128)} %copy.135), channel_id=1, source_target_pairs={{0,1},{1,0},{2,3},{3,2},{4,5},{5,4},{6,7},{7,6},{8,9},{9,8},{10,11... | collective-permute-start | bytes 55304 | tf_op jit(solution)/shard_map/ppermute | solution.py:16
  25.0 178.5 %collective-permute-start.3 = (bf16[64,1536]{0,1:T(8,128)(2,1)}, bf16[64,1536]{0,1:T(8,128)(2,1)S(1)}, u32[]{:S(2)}, u32[]{:S(2)}) collective-permute-start(bf16[64,1536]{0,1:T(8,128)(2,1)} %bitcast.46), channel_id=1, source_target_pairs={{0,1},{1,0},{2,3},{3,2},{4,5},{5,4},{6,7},{7,6},{8,9},{9,8},{10,11... | collective-permute-start | bytes 589832 | tf_op jit(solution)/shard_map/ppermute | solution.py:16
  25.6 48.4 %copy-start.20 = (s32[6144,1]{0,1:T(1,128)}, s32[6144,1]{0,1:T(1,128)S(1)}, u32[]{:S(2)}) copy-start(s32[6144,1]{0,1:T(1,128)S(1)} %get-tuple-element.893) | copy-start | bytes 73732
  26.4 47.7 %copy-start.24 = (s32[2048,1]{0,1:T(1,128)}, s32[2048,1]{0,1:T(1,128)S(1)}, u32[]{:S(2)}) copy-start(s32[2048,1]{0,1:T(1,128)S(1)} %get-tuple-element.902) | copy-start | bytes 24580
  150.6 3.1 copy-start.3
  178.9 6.6 copy-start
  178.9 6.6 copy-start.1
  178.9 6.6 copy-start.8
  178.9 6.6 copy-start.9
  178.9 6.6 copy-start.10
  178.9 6.6 copy-start.18
  179.0 6.6 copy-start.25
  179.0 6.6 copy-start.27
  203.5 6.2 copy-start.12
  203.5 6.4 copy-start.4
  251.7 14.4 %copy-start.5 = (f32[64,2048]{1,0:T(8,128)}, f32[64,2048]{1,0:T(8,128)S(1)}, u32[]{:S(2)}) copy-start(f32[64,2048]{1,0:T(8,128)S(1)} %get-tuple-element.376) | copy-start | bytes 1572868
  251.7 14.4 %copy-start.14 = (f32[3,2048]{1,0:T(4,128)}, f32[3,2048]{1,0:T(4,128)S(1)}, u32[]{:S(2)}) copy-start(f32[3,2048]{1,0:T(4,128)S(1)} %get-tuple-element.370) | copy-start | bytes 73732
  251.7 14.4 %copy-start.16 = (f32[3,2048]{1,0:T(4,128)}, f32[3,2048]{1,0:T(4,128)S(1)}, u32[]{:S(2)}) copy-start(f32[3,2048]{1,0:T(4,128)S(1)} %get-tuple-element.372) | copy-start | bytes 73732
  266.1 478.9 %collective-permute-start.6 = (f32[64,1536]{1,0:T(8,128)}, f32[64,1536]{1,0:T(8,128)}, u32[]{:S(2)}, u32[]{:S(2)}) collective-permute-start(f32[64,1536]{1,0:T(8,128)} %copy.163), channel_id=1, source_target_pairs={{0,2},{2,4},{4,6},{6,8},{8,10},{10,12},{12,14},{14,16},{16,18},{18... | collective-permute-start | bytes 1179656 | tf_op jit(solution)/shard_map/ppermute | solution.py:16
  266.2 13.2 %copy-start.13 = (f32[3,2048]{1,0:T(4,128)S(1)}, f32[3,2048]{1,0:T(4,128)}, u32[]{:S(2)}) copy-start(f32[3,2048]{1,0:T(4,128)} %copy-done.12) | copy-start | bytes 73732
  279.3 13.0 %copy-start.17 = (f32[3,2048]{1,0:T(4,128)S(1)}, f32[3,2048]{1,0:T(4,128)}, u32[]{:S(2)}) copy-start(f32[3,2048]{1,0:T(4,128)} %copy-done.16) | copy-start | bytes 73732
  279.3 467.0 %collective-permute-start.7 = (f32[64,1536]{1,0:T(8,128)}, f32[64,1536]{1,0:T(8,128)}, u32[]{:S(2)}, u32[]{:S(2)}) collective-permute-start(f32[64,1536]{1,0:T(8,128)} %copy.166), channel_id=1, source_target_pairs={{0,1},{1,0},{2,3},{3,2},{4,5},{5,4},{6,7},{7,6},{8,9},{9,8},{10,11... | collective-permute-start | bytes 1179656 | tf_op jit(solution)/shard_map/ppermute | solution.py:16
  292.4 429.8 %collective-permute-start.4 = (f32[3,1536]{1,0:T(4,128)}, f32[3,1536]{1,0:T(4,128)}, u32[]{:S(2)}, u32[]{:S(2)}) collective-permute-start(f32[3,1536]{1,0:T(4,128)} %copy.153), channel_id=1, source_target_pairs={{0,2},{2,4},{4,6},{6,8},{8,10},{10,12},{12,14},{14,16},{16,18},{18... | collective-permute-start | bytes 55304 | tf_op jit(solution)/shard_map/ppermute | solution.py:16
  305.4 417.8 %collective-permute-start.5 = (f32[3,1536]{1,0:T(4,128)}, f32[3,1536]{1,0:T(4,128)}, u32[]{:S(2)}, u32[]{:S(2)}) collective-permute-start(f32[3,1536]{1,0:T(4,128)} %copy.156), channel_id=1, source_target_pairs={{0,1},{1,0},{2,3},{3,2},{4,5},{5,4},{6,7},{7,6},{8,9},{9,8},{10,11... | collective-permute-start | bytes 55304 | tf_op jit(solution)/shard_map/ppermute | solution.py:16
  667.8 3.8 copy-start.15
  (9 other events, 20.1 us)
where the time goes:
time: 779 us; the launch traced here: 769 us
  other arithmetic  323 us (41%)
  local copies, waits for them, and re-layouts  230 us (30%)
  matrix products  134 us (17%)
  blocking collectives  53.5 us (7%)
  loops' own time  12.8 us (2%)
  starting transfers between devices  10.3 us (1%)
    scatter-add x2, other arithmetic, on_device(): jnp.zeros((3, atoms), jnp.float32).at[:, source].add(grads[0]).at[:, target]  67.6 us
    scatter-add x2, other arithmetic, on_device(): grad_feat = jnp.zeros((width, atoms), jnp.float32).at[:, source].add(grad...  67.6 us
    psum x1, blocking collectives, on_device(): total = lax.psum(energy_loc + energy_x + energy_y, ('gx', 'gy'))  53.5 us
    dot_general x36, matrix products, pair_energy(): jnp.dot(w_hidden.T, hidden, preferred_element_type=jnp.float32)  52.9 us
    while x16, local copies, waits for them, and re-layouts, run_edges(): lax.fori_loop(0, filled, visit_live, (jnp.zeros((), jnp.float32), start_g...  27.8 us
    dot_general x36, matrix products, pair_energy(): jnp.dot(w_dst.T, dst_feat.astype(jnp.bfloat16), preferred_element_type=jn...  26.5 us
    gather x1, local copies, waits for them, and re-layouts, on_device(): features[:, source]  22.1 us
    gather x1, local copies, waits for them, and re-layouts, on_device(): features[:, target]  22 us
  transfers between devices with their start and end apart: 8, of which 0 were waited for; matrix products, arithmetic and copies ran while one was open for 78% of the time, Pallas kernels for 0%

commit v1 on v0

v1 whole, which is shorter than its diff:
```python
import functools
import math

import jax
import jax.numpy as jnp
from jax import lax
from jax.experimental import pallas as pl
from jax.experimental.pallas import tpu as pltpu
from jax.sharding import PartitionSpec as P

BLOCK = 512
GROUPS = 4
FIRST_SHARE = 4

cutoff_radius = 6.0
block_edge = 6.0
softening = 0.1

F32 = jnp.float32
BF16 = jnp.bfloat16


def shifted(array, axis, by):
    length = lax.axis_size(axis)
    return lax.ppermute(array, axis, [(i, (i + by) % length) for i in range(length)])


def sin_cos_pi(x):
    near = jnp.floor(x + 0.5)
    y = (x - near) * math.pi
    odd = near - 2.0 * jnp.floor(near * 0.5)
    sign = 1.0 - 2.0 * odd
    z = y * y
    s = z * (-1.0 / 39916800) + 1.0 / 362880
    s = s * z - 1.0 / 5040
    s = s * z + 1.0 / 120
    s = s * z - 1.0 / 6
    s = s * z + 1.0
    c = z * (1.0 / 479001600) - 1.0 / 3628800
    c = c * z + 1.0 / 40320
    c = c * z - 1.0 / 720
    c = c * z + 1.0 / 24
    c = c * z - 0.5
    c = c * z + 1.0
    return sign * (s * y), sign * c


def group_of(index, size, groups):
    group = jnp.zeros_like(index)
    for g in range(1, groups):
        group = group + (index >= g * size).astype(jnp.int32)
    return group, index - group * size


def pick_group(stack, group, height, groups, base=0):
    out = stack[base + (groups - 1) * height : base + groups * height]
    for g in range(groups - 2, -1, -1):
        out = jnp.where(group == g, stack[base + g * height : base + (g + 1) * height], out)
    return out


def one_hot(row, size):
    spots = lax.broadcasted_iota(jnp.int32, (size, row.shape[1]), 0)
    return jnp.where(spots == row, 1.0, 0.0).astype(BF16)


def fill_table(table, wide, feat, pos):
    width = feat.shape[0]
    size = table.shape[1]
    p = pos[...]
    high = p.astype(BF16).astype(F32)
    low = p - high
    wide[...] = jnp.zeros_like(wide)
    for g in range(GROUPS):
        span = slice(g * size, (g + 1) * size)
        table[g * width : (g + 1) * width, :] = feat[:, span]
        wide[8 * g : 8 * g + 3, :] = high[:, span]
        wide[8 * g + 3 : 8 * g + 6, :] = low[:, span]
    table[GROUPS * width :, :] = wide[...].astype(BF16)


def block_work(
    indices, begin, count, offset, tab_src, tab_dst, weights, scratch, energy, width, nrbf, nspec
):
    fwd_in, fwd_hid, bwd_hid, bwd_in, readout = weights
    hots, grads, inputs = scratch
    src, dst, kind_src, kind_dst = indices
    size = tab_src.shape[1]
    lanes = src.shape[1]
    base = GROUPS * width
    grp_src, row_src = group_of(src, size, GROUPS)
    grp_dst, row_dst = group_of(dst, size, GROUPS)
    hots[:, 0:lanes] = one_hot(row_src, size)
    hots[:, lanes : 2 * lanes] = one_hot(row_dst, size)
    got_src = jnp.dot(tab_src[...], hots[:, 0:lanes], preferred_element_type=F32)
    got_dst = jnp.dot(tab_dst[...], hots[:, lanes : 2 * lanes], preferred_element_type=F32)
    inputs[0:width, :] = pick_group(got_src, grp_src, width, GROUPS).astype(BF16)
    inputs[width : 2 * width, :] = pick_group(got_dst, grp_dst, width, GROUPS).astype(BF16)
    gap = pick_group(got_dst, grp_dst, 8, GROUPS, base) - pick_group(
        got_src, grp_src, 8, GROUPS, base
    )
    sub = lax.broadcasted_iota(jnp.int32, (8, lanes), 0)
    gap = gap + pltpu.roll(gap, 5, 0)
    if offset is not None:
        gap = gap + jnp.where(sub == offset, block_edge, 0.0)
    gap = jnp.where(sub < 3, gap, 0.0)
    radius = jnp.sqrt(jnp.sum(gap * gap, axis=0, keepdims=True) + softening)
    inverse = 1.0 / radius
    ratio = jnp.minimum(radius * (1.0 / cutoff_radius), 1.0)
    inside = 1.0 - ratio * ratio
    slots = begin + lax.broadcasted_iota(jnp.int32, (1, lanes), 1)
    live = jnp.where(slots < count, 1.0, 0.0)
    weight = inside * inside * live
    orders = (sub + 1).astype(F32)
    sines, cosines = sin_cos_pi(orders * ratio)
    basis = sines * inverse
    slope = (orders * (math.pi / cutoff_radius) * cosines - basis) * inverse
    kinds = jnp.where(sub < nspec, kind_src, kind_dst + nspec)
    inputs[2 * width :, :] = jnp.concatenate(
        [basis, jnp.where(sub == kinds, 1.0, 0.0)], axis=0
    ).astype(BF16)

    half = jnp.dot(fwd_in[...], inputs[...], preferred_element_type=F32)
    tan = jnp.tanh(half)
    up = 1.0 + tan
    hidden = half * up
    slope_one = up + hidden * (1.0 - tan)
    half = jnp.dot(fwd_hid[...], hidden.astype(BF16), preferred_element_type=F32)
    tan = jnp.tanh(half)
    up = 1.0 + tan
    second = half * up
    slope_two = up + second * (1.0 - tan)
    read = readout[...]
    score = jnp.concatenate(
        [
            jnp.sum(second[:, c : c + 128] * read, axis=0, keepdims=True)
            for c in range(0, lanes, 128)
        ],
        axis=1,
    )
    energy[...] += weight * score
    back = jnp.dot(bwd_hid[...], slope_two.astype(BF16), preferred_element_type=F32)
    back = (back * slope_one).astype(BF16)
    back = jnp.dot(bwd_in[...], back, preferred_element_type=F32)
    scale = 0.25 * weight
    radial = scale * jnp.sum(back[2 * width : 2 * width + nrbf] * slope, axis=0, keepdims=True)
    radial = radial - (4.0 / cutoff_radius) * (inside * ratio * live) * score
    push = (gap * (radial * inverse)).astype(F32)
    for side, (group, part, move) in enumerate(
        (
            (grp_src, back[0:width] * scale, -push),
            (grp_dst, back[width : 2 * width] * scale, push),
        )
    ):
        span = slice(side * lanes, (side + 1) * lanes)
        part = part.astype(BF16)
        moves = []
        for g in range(GROUPS):
            mask = jnp.where(group == g, 1.0, 0.0)
            grads[g * width : (g + 1) * width, span] = part * mask.astype(BF16)
            moves.append(move * mask)
        grads[base:, span] = jnp.concatenate(moves, axis=0).astype(BF16)


def scatter(total, grads, hots, span):
    total[...] += lax.dot_general(
        grads[:, span], hots[:, span], (((1,), (1,)), ((), ())), preferred_element_type=F32
    )


def rows_of(pairs, begin):
    span = pl.ds(pl.multiple_of(begin, BLOCK), BLOCK)
    return [pairs[k : k + 1, span] for k in range(4)]


def local_kernel(
    first,
    dims,
    counts,
    pairs,
    *refs,
):
    width, nrbf, nspec = dims
    lanes = BLOCK
    if first:
        (feat, pos, w_rbf, w_src, w_dst, sp_src, sp_dst, w_hid, w_lat, w_en) = refs[:10]
        (total, energy, table, fwd_in, fwd_hid, bwd_hid, bwd_in, readout) = refs[10:18]
        hots, grads, inputs, wide, runs = refs[18:]
        fill_table(table, wide, feat, pos)
        full = jnp.concatenate(
            [ref[...].astype(F32) for ref in (w_src, w_dst, w_rbf)]
            + [jnp.concatenate([sp_src[...].astype(F32), sp_dst[...].astype(F32)], axis=0)],
            axis=0,
        )
        bwd_in[...] = full.astype(BF16)
        fwd_in[...] = (0.5 * full.T).astype(BF16)
        hid = w_hid[...].astype(F32)
        fwd_hid[...] = (0.5 * hid.T).astype(BF16)
        column = jnp.sum(w_lat[...].astype(F32) * w_en[...], axis=1, keepdims=True)
        spread = jnp.broadcast_to(column, (column.shape[0], 128))
        readout[...] = spread
        bwd_hid[...] = (hid * spread.T[0:1, :]).astype(BF16)
        total[...] = jnp.zeros_like(total)
        energy_in = None
    else:
        (total_in, energy_in, table, fwd_in, fwd_hid, bwd_hid, bwd_in, readout) = refs[:8]
        total, energy = refs[8:10]
        hots, grads, inputs, runs = refs[10:]
        total[...] = total_in[...]
    runs[...] = jnp.zeros_like(runs)
    count = counts[0, 0]
    filled = (count + BLOCK - 1) // BLOCK
    low = 0 if first else jnp.minimum(filled, FIRST_SHARE)
    high = jnp.minimum(filled, FIRST_SHARE) if first else filled
    weights = (fwd_in, fwd_hid, bwd_hid, bwd_in, readout)

    def visit(index, carry):
        begin = index * BLOCK
        block_work(
            rows_of(pairs, begin),
            begin,
            count,
            None,
            table,
            table,
            weights,
            (hots, grads, inputs),
            runs,
            width,
            nrbf,
            nspec,
        )
        scatter(total, grads, hots, slice(0, 2 * lanes))
        return carry

    lax.fori_loop(low, high, visit, 0)
    fold_energy(energy, runs, energy_in)


def fold_energy(energy, runs, energy_in):
    part = jnp.sum(runs[...], axis=1, keepdims=True)
    part = jnp.broadcast_to(part, energy.shape)
    energy[...] = part if energy_in is None else part + energy_in[...]


def cross_kernel(
    dims,
    counts,
    pairs_x,
    pairs_y,
    feat_x,
    pos_x,
    lists_x,
    feat_y,
    pos_y,
    lists_y,
    total_in,
    energy_in,
    table,
    fwd_in,
    fwd_hid,
    bwd_hid,
    bwd_in,
    readout,
    total,
    energy,
    back_x,
    back_y,
    hots,
    grads,
    inputs,
    wide,
    runs,
    other,
    away,
    lent,
):
    width, nrbf, nspec = dims
    lanes = BLOCK
    size = table.shape[1]
    parts = lists_x.shape[1] // size
    weights = (fwd_in, fwd_hid, bwd_hid, bwd_in, readout)
    total[...] = total_in[...]
    runs[...] = jnp.zeros_like(runs)
    for axis, (pairs, feat, pos, lists, back) in enumerate(
        ((pairs_x, feat_x, pos_x, lists_x, back_x), (pairs_y, feat_y, pos_y, lists_y, back_y))
    ):
        fill_table(other, wide, feat, pos)
        away[...] = jnp.zeros_like(away)
        wide[...] = jnp.zeros_like(wide)
        for g in range(parts):
            ids = lists[axis : axis + 1, g * size : (g + 1) * size]
            wide[2 * g : 2 * g + 1, :] = (ids >> 6).astype(F32)
            wide[2 * g + 1 : 2 * g + 2, :] = (ids & 63).astype(F32)
        lent[...] = wide[0 : lent.shape[0], :].astype(BF16)
        count = counts[0, 1 + axis]

        def visit(index, carry):
            begin = index * BLOCK
            src, slot, kind_src, kind_dst = rows_of(pairs, begin)
            grp, row = group_of(slot, size, parts)
            found = jnp.dot(lent[...], one_hot(row, size), preferred_element_type=F32)
            found = pick_group(found, grp, 2, parts)
            dst = (found[0:1] * 64.0 + found[1:2]).astype(jnp.int32)
            block_work(
                (src, dst, kind_src, kind_dst),
                begin,
                count,
                axis,
                table,
                other,
                weights,
                (hots, grads, inputs),
                runs,
                width,
                nrbf,
                nspec,
            )
            scatter(total, grads, hots, slice(0, lanes))
            scatter(away, grads, hots, slice(lanes, 2 * lanes))
            return carry

        lax.fori_loop(0, (count + BLOCK - 1) // BLOCK, visit, 0)
        back[...] = away[...].astype(BF16)
    fold_energy(energy, runs, energy_in)


def join_kernel(total, back_x, back_y, forces, feature_grads):
    width = feature_grads.shape[0]
    size = total.shape[1]
    base = GROUPS * width
    for g in range(GROUPS):
        span = slice(g * size, (g + 1) * size)
        rows = slice(g * width, (g + 1) * width)
        feature_grads[:, span] = total[rows] + (
            back_x[rows].astype(F32) + back_y[rows].astype(F32)
        )
    moved = total[base:] + (back_x[base:].astype(F32) + back_y[base:].astype(F32))
    for g in range(GROUPS):
        forces[:, g * size : (g + 1) * size] = -moved[8 * g : 8 * g + 3]


def on_device(
    positions,
    features,
    halo_lists,
    local_pairs,
    cross_x,
    cross_y,
    pair_counts,
    w_rbf,
    w_src,
    w_dst,
    species_src,
    species_dst,
    w_hidden,
    w_latent,
    w_energy,
):
    atoms = positions.shape[1]
    width = features.shape[0]
    nrbf, hid = w_rbf.shape
    nspec = species_src.shape[0]
    size = atoms // GROUPS
    tall = GROUPS * (width + 8)
    depth = 2 * width + nrbf + 2 * nspec
    dims = (width, nrbf, nspec)
    got = [
        [shifted(item, axis, -1) for item in (features, positions, halo_lists)]
        for axis in ("gx", "gy")
    ]
    vmem = pl.BlockSpec(memory_space=pltpu.VMEM)
    smem = pl.BlockSpec(memory_space=pltpu.SMEM)
    shape = jax.ShapeDtypeStruct
    scratch = [
        pltpu.VMEM((size, 2 * BLOCK), BF16),
        pltpu.VMEM((tall, 2 * BLOCK), BF16),
        pltpu.VMEM((depth, BLOCK), BF16),
    ]
    wide = pltpu.VMEM((GROUPS * 8, size), F32)
    runs = pltpu.VMEM((1, BLOCK), F32)
    total_like = shape((tall, size), F32)
    energy_like = shape((1, 128), F32)
    params = pltpu.CompilerParams(vmem_limit_bytes=48 * 1024 * 1024)
    prepared = (
        shape((tall, size), BF16),
        shape((hid, depth), BF16),
        shape((hid, hid), BF16),
        shape((hid, hid), BF16),
        shape((depth, hid), BF16),
        shape((hid, 128), F32),
    )
    total, energy, *shared = pl.pallas_call(
        functools.partial(local_kernel, True, dims),
        out_shape=(total_like, energy_like) + prepared,
        in_specs=[smem] + [vmem] * 11,
        out_specs=[vmem] * 8,
        scratch_shapes=scratch + [wide, runs],
        compiler_params=params,
        name="local_first",
    )(
        pair_counts,
        local_pairs,
        features,
        positions,
        w_rbf,
        w_src,
        w_dst,
        species_src,
        species_dst,
        w_hidden,
        w_latent,
        w_energy.reshape(1, -1),
    )
    total, energy, back_x, back_y = pl.pallas_call(
        functools.partial(cross_kernel, dims),
        out_shape=(total_like, energy_like, shape((tall, size), BF16), shape((tall, size), BF16)),
        in_specs=[smem] + [vmem] * 16,
        out_specs=[vmem] * 4,
        scratch_shapes=scratch
        + [
            wide,
            runs,
            pltpu.VMEM((tall, size), BF16),
            pltpu.VMEM((tall, size), F32),
            pltpu.VMEM((16, size), BF16),
        ],
        compiler_params=params,
        name="cross",
    )(pair_counts, cross_x, cross_y, *got[0], *got[1], total, energy, *shared)
    back_x = shifted(back_x, "gx", 1)
    back_y = shifted(back_y, "gy", 1)
    total, energy = pl.pallas_call(
        functools.partial(local_kernel, False, dims),
        out_shape=(total_like, energy_like),
        in_specs=[smem] + [vmem] * 9,
        out_specs=[vmem] * 2,
        scratch_shapes=scratch + [runs],
        compiler_params=params,
        name="local_rest",
    )(pair_counts, local_pairs, total, energy, *shared)
    forces, feature_grads = pl.pallas_call(
        join_kernel,
        out_shape=(shape(positions.shape, F32), shape(features.shape, F32)),
        in_specs=[vmem] * 3,
        out_specs=[vmem] * 2,
        compiler_params=params,
        name="join",
    )(total, back_x, back_y)
    summed = lax.psum(energy[0, 0], ("gx", "gy"))
    atoms_all = atoms * lax.axis_size("gx") * lax.axis_size("gy")
    return ((summed / atoms_all).reshape(1), forces, feature_grads)


def solution(mesh):
    spread = P(None, ("gx", "gy"))
    return jax.shard_map(
        on_device,
        mesh=mesh,
        in_specs=(spread,) * 6 + (P(("gx", "gy"), None),) + (P(),) * 8,
        out_specs=(P(), spread, spread),
        check_vma=False,
    )
```

time: 779 us -> 107 us (0.14); the launches traced: 769 us -> 105 us
  other arithmetic: 323 us -> 0 us
  local copies, waits for them, and re-layouts: 230 us -> 7.71 us
  matrix products: 134 us -> 0 us
  Pallas kernels: 0 us -> 38.8 us
  blocking collectives: 53.5 us -> 40 us
  loops' own time: 12.8 us -> 0 us
    scatter-add x16 -> x0, other arithmetic: 268 us -> none  [the longest x2 67.6 us: on_device(): jnp.zeros((3, atoms), jnp.float32).at[:, source].add(grads[0]).at[:, target]]
    gather x18 -> x0, local copies, waits for them, and re-layouts: 157 us -> none  [the longest x1 22.1 us: on_device(): features[:, source]]
    dot_general x216 -> x0, matrix products: 134 us -> none  [the longest x36 52.9 us: pair_energy(): jnp.dot(w_hidden.T, hidden, preferred_element_type=jnp.float32)]
    pallas_call x0 -> x4, Pallas kernels: none -> 38.8 us  [the longest x1 16.1 us: on_device(): pl.pallas_call(functools.partial(local_kernel, False, dims), out_shape=(t...]
    while x24 -> x0, local copies, waits for them, and re-layouts: 27.9 us -> none  [the longest x16 27.8 us: run_edges(): lax.fori_loop(0, filled, visit_live, (jnp.zeros((), jnp.float32), start_g...]
    dynamic_slice x36 -> x0, local copies, waits for them, and re-layouts: 21.9 us -> none  [visit_live(): lax.dynamic_slice_in_dim(item, begin, BLOCK, axis=item.ndim - 1)]
    mul x36 -> x0, other arithmetic: 20.6 us -> none  [the longest x18 20.5 us: pair_energy(): radius = jnp.sqrt(jnp.sum(displace * displace, axis=0) + softening)]
    psum x1, blocking collectives: 53.5 us -> 40 us  [on_device(): summed = lax.psum(energy[0, 0], ('gx', 'gy'))]
  transfers between devices with their start and end apart: 8 -> 8, of which waited for: 0 -> 1; matrix products, arithmetic and copies ran while one was open for 78% -> 1% of each run, Pallas kernels for 0% -> 24%
where the time goes in v1:
time: 107 us; the launch traced here: 105 us
  blocking collectives  40 us (37%)
  Pallas kernels  38.8 us (36%)
  starting transfers between devices  12.6 us (12%)
  local copies, waits for them, and re-layouts  7.71 us (7%)
  waiting for transfers between devices  3.45 us (3%)
  between operations  2.52 us (2%)
    psum x1, blocking collectives, on_device(): summed = lax.psum(energy[0, 0], ('gx', 'gy'))  40 us
    pallas_call x1, Pallas kernels, on_device(): pl.pallas_call(functools.partial(local_kernel, False, dims), out_shape=(t...  16.1 us
    pallas_call x1, Pallas kernels, on_device(): pl.pallas_call(functools.partial(cross_kernel, dims), out_shape=(total_li...  13.2 us
    ppermute x8, starting transfers between devices, shifted(): lax.ppermute(array, axis, [(i, (i + by) % length) for i in range(length)])  12.6 us
    pallas_call x1, Pallas kernels, on_device(): pl.pallas_call(functools.partial(local_kernel, True, dims), out_shape=(to...  8.63 us
    unnamed x27, local copies, waits for them, and re-layouts  7.71 us
    ppermute x8, waiting for transfers between devices, shifted(): lax.ppermute(array, axis, [(i, (i + by) % length) for i in range(length)])  3.45 us
  transfers between devices with their start and end apart: 8, of which 1 were waited for; matrix products, arithmetic and copies ran while one was open for 1% of the time, Pallas kernels for 24%

profile of v1, /device:TPU:0, one launch (start us, length us, event | category | flops | bytes accessed | tf_op | source)
XLA Modules:
  0.0 105.1 jit_solution(935182472773884781)
XLA Ops:
  0.6 5.5 %collective-permute-start = (bf16[64,2048]{1,0:T(8,128)(2,1)}, bf16[64,2048]{1,0:T(8,128)(2,1)S(1)}, u32[]{:S(2)}, u32[]{:S(2)}) collective-permute-start(bf16[64,2048]{1,0:T(8,128)(2,1)} %refs_0_.1), channel_id=1, source_target_pairs={{0,30},{2,0},{4,2},{6,4},{8,6},{10,8},{12,10},{14,12},{16,14},{18,... | collective-permute-start | bytes 786440 | tf_op jit(solution)/shard_map/ppermute | solution.py:25
  6.2 1.5 %collective-permute-start.3 = (bf16[64,2048]{1,0:T(8,128)(2,1)}, bf16[64,2048]{1,0:T(8,128)(2,1)S(1)}, u32[]{:S(2)}, u32[]{:S(2)}) collective-permute-start(bf16[64,2048]{1,0:T(8,128)(2,1)} %refs_0_.1), channel_id=1, source_target_pairs={{0,1},{1,0},{2,3},{3,2},{4,5},{5,4},{6,7},{7,6},{8,9},{9,8},{10,11... | collective-permute-start | bytes 786440 | tf_op jit(solution)/shard_map/ppermute | solution.py:25
  7.7 0.5 collective-permute-start.5
  8.2 0.1 collective-permute-start.1
  8.3 1.5 %collective-permute-start.4 = (f32[3,2048]{1,0:T(4,128)}, f32[3,2048]{1,0:T(4,128)S(1)}, u32[]{:S(2)}, u32[]{:S(2)}) collective-permute-start(f32[3,2048]{1,0:T(4,128)} %refs_1_.1), channel_id=1, source_target_pairs={{0,1},{1,0},{2,3},{3,2},{4,5},{5,4},{6,7},{7,6},{8,9},{9,8},{10,11... | collective-permute-start | bytes 73736 | tf_op jit(solution)/shard_map/ppermute | solution.py:25
  9.8 3.4 %collective-permute-done.5.lists_y = s32[2,1536]{1,0:T(2,128)S(1)} collective-permute-done((s32[2,1536]{1,0:T(2,128)}, s32[2,1536]{1,0:T(2,128)S(1)}, u32[]{:S(2)}, u32[]{:S(2)}) %collective-permute-start.5) | collective-permute-done | bytes 12320 | tf_op jit(solution)/shard_map/ppermute | solution.py:25
  13.2 1.9 %collective-permute-start.2 = (s32[2,1536]{1,0:T(2,128)}, s32[2,1536]{1,0:T(2,128)S(1)}, u32[]{:S(2)}, u32[]{:S(2)}) collective-permute-start(s32[2,1536]{1,0:T(2,128)} %param.17), channel_id=1, source_target_pairs={{0,30},{2,0},{4,2},{6,4},{8,6},{10,8},{12,10},{14,12},{16,14},{18,... | collective-permute-start | bytes 36872 | tf_op jit(solution)/shard_map/ppermute | solution.py:25
  15.1 0.9 copy.18.refs_8_
  16.0 0.0 copy-start.8
  16.0 0.0 copy-start.12
  16.0 0.6 copy-done.8
  16.6 0.0 copy-done.12
  16.7 0.9 copy-done.1
  17.6 0.9 copy-done.2
  18.5 0.8 copy-done.5
  19.3 0.8 copy-done.6
  20.0 0.8 copy-done.7
  20.8 0.7 copy-done.9
  21.5 0.7 copy-done.10
  22.2 0.7 copy-done.11
  22.8 8.6 %local_first.1 = (f32[288,512]{1,0:T(8,128)S(1)}, f32[1,128]{1,0:T(1,128)S(1)}, bf16[288,512]{1,0:T(8,128)(2,1)S(1)}, bf16[256,144]{1,0:T(8,128)(2,1)S(1)}, bf16...) custom-call(s32[1,3]{1,0:T(1,128)S(1)} %copy-done.8, ...), custom_call_target="tpu_custom_call" | custom-call | tf_op jit(solution)/shard_map/local_first/pallas_call | solution.py:393
  31.5 0.0 collective-permute-done.2.lists_x
  31.5 0.0 collective-permute-done.1.pos_x
  31.5 0.0 collective-permute-done.4.pos_y
  31.5 0.0 collective-permute-done.feat_x
  31.5 13.2 %cross.1 = (f32[288,512]{1,0:T(8,128)S(1)}, f32[1,128]{1,0:T(1,128)S(1)}, bf16[288,512]{1,0:T(8,128)(2,1)S(1)}, bf16[288,512]{1,0:T(8,128)(2,1)S(1)}) custom-call(s32[1,3]{1,0:T(1,128)S(1)} %copy-done.8, s32[4,2048]{1,0:T(4,128)S(1)} %copy-done.3, s32[4,2048]{1,0:T(4,128)S(1)} %copy-done.4, bf16[64,2048]{1,0:T(8,128)(2,1)S(1)} %collective-permute-done.feat_x, ...), custom_call_target="tpu_custom_call" | custom-call | tf_op jit(solution)/shard_map/cross/pallas_call | solution.py:415
  44.7 0.0 collective-permute-start.6
  44.7 1.6 %collective-permute-start.7 = (bf16[288,512]{1,0:T(8,128)(2,1)S(1)}, bf16[288,512]{1,0:T(8,128)(2,1)S(1)}, u32[]{:S(2)}, u32[]{:S(2)}) collective-permute-start(bf16[288,512]{1,0:T(8,128)(2,1)S(1)} %get-tuple-element.32), channel_id=1, source_target_pairs={{0,1},{1,0},{2,3},{3,2},{4,5},{5,4},{6,7},{7,6},{8,9},{9,8},{10,11... | collective-permute-start | bytes 884744 | tf_op jit(solution)/shard_map/ppermute | solution.py:25
  46.3 16.1 %local_rest.1 = (f32[288,512]{1,0:T(8,128)S(1)}, f32[1,128]{1,0:T(1,128)S(1)}) custom-call(s32[1,3]{1,0:T(1,128)S(1)} %copy-done.8, s32[4,6144]{1,0:T(4,128)S(1)} %copy-done, f32[288,512]{1,0:T(8,128)S(1)} %get-tuple-element.27.refs_0_, f32[1,128]{1,0:T(1,128)S(1)} %get-tuple-element.28.refs_1_, bf16[288,512]{1,0:T(8,128)(2,1)S(1)} %get-tuple-element.21.table.refs_2_, ...), custom_call_target="tpu_custom_call" | custom-call | tf_op jit(solution)/shard_map/local_rest/pallas_call | solution.py:433
  62.4 40.0 %psum.7 = f32[]{:T(128)} all-reduce(f32[]{:T(128)S(1)} %bitcast.5), channel_id=1, replica_groups=mesh['gx'=16,'gy'=2] {'gx','gy'}, use_global_device_ids=true, to_apply=%region_0.0 | all-reduce | flops 1 | bytes 8 | tf_op jit(solution)/shard_map/psum | solution.py:450
  103.1 0.0 collective-permute-done.7.back_y
  103.1 0.9 join.1
  (16 shorter events, 0.0 us)
Async XLA Ops:
  0.6 15.4 %copy-start = (s32[4,6144]{1,0:T(4,128)S(1)}, s32[4,6144]{1,0:T(4,128)}, u32[]{:S(2)}) copy-start(s32[4,6144]{1,0:T(4,128)} %pairs.3) | copy-start | bytes 294916
  0.6 30.8 %collective-permute-start = (bf16[64,2048]{1,0:T(8,128)(2,1)}, bf16[64,2048]{1,0:T(8,128)(2,1)S(1)}, u32[]{:S(2)}, u32[]{:S(2)}) collective-permute-start(bf16[64,2048]{1,0:T(8,128)(2,1)} %refs_0_.1), channel_id=1, source_target_pairs={{0,30},{2,0},{4,2},{6,4},{8,6},{10,8},{12,10},{14,12},{16,14},{18,... | collective-permute-start | bytes 786440 | tf_op jit(solution)/shard_map/ppermute | solution.py:25
  6.2 25.3 %collective-permute-start.3 = (bf16[64,2048]{1,0:T(8,128)(2,1)}, bf16[64,2048]{1,0:T(8,128)(2,1)S(1)}, u32[]{:S(2)}, u32[]{:S(2)}) collective-permute-start(bf16[64,2048]{1,0:T(8,128)(2,1)} %refs_0_.1), channel_id=1, source_target_pairs={{0,1},{1,0},{2,3},{3,2},{4,5},{5,4},{6,7},{7,6},{8,9},{9,8},{10,11... | collective-permute-start | bytes 786440 | tf_op jit(solution)/shard_map/ppermute | solution.py:25
  7.7 5.6 %collective-permute-start.5 = (s32[2,1536]{1,0:T(2,128)}, s32[2,1536]{1,0:T(2,128)S(1)}, u32[]{:S(2)}, u32[]{:S(2)}) collective-permute-start(s32[2,1536]{1,0:T(2,128)} %param.17), channel_id=1, source_target_pairs={{0,1},{1,0},{2,3},{3,2},{4,5},{5,4},{6,7},{7,6},{8,9},{9,8},{10,11... | collective-permute-start | bytes 36872 | tf_op jit(solution)/shard_map/ppermute | solution.py:25
  8.2 23.3 %collective-permute-start.1 = (f32[3,2048]{1,0:T(4,128)}, f32[3,2048]{1,0:T(4,128)S(1)}, u32[]{:S(2)}, u32[]{:S(2)}) collective-permute-start(f32[3,2048]{1,0:T(4,128)} %refs_1_.1), channel_id=1, source_target_pairs={{0,30},{2,0},{4,2},{6,4},{8,6},{10,8},{12,10},{14,12},{16,14},{18,... | collective-permute-start | bytes 73736 | tf_op jit(solution)/shard_map/ppermute | solution.py:25
  8.3 23.2 %collective-permute-start.4 = (f32[3,2048]{1,0:T(4,128)}, f32[3,2048]{1,0:T(4,128)S(1)}, u32[]{:S(2)}, u32[]{:S(2)}) collective-permute-start(f32[3,2048]{1,0:T(4,128)} %refs_1_.1), channel_id=1, source_target_pairs={{0,1},{1,0},{2,3},{3,2},{4,5},{5,4},{6,7},{7,6},{8,9},{9,8},{10,11... | collective-permute-start | bytes 73736 | tf_op jit(solution)/shard_map/ppermute | solution.py:25
  13.2 18.2 %collective-permute-start.2 = (s32[2,1536]{1,0:T(2,128)}, s32[2,1536]{1,0:T(2,128)S(1)}, u32[]{:S(2)}, u32[]{:S(2)}) collective-permute-start(s32[2,1536]{1,0:T(2,128)} %param.17), channel_id=1, source_target_pairs={{0,30},{2,0},{4,2},{6,4},{8,6},{10,8},{12,10},{14,12},{16,14},{18,... | collective-permute-start | bytes 36872 | tf_op jit(solution)/shard_map/ppermute | solution.py:25
  16.0 0.7 copy-start.8
  16.0 0.7 copy-start.12
  16.7 0.9 copy-start.1
  17.6 0.9 copy-start.2
  18.5 0.8 copy-start.5
  19.3 0.8 copy-start.6
  20.0 0.8 copy-start.7
  20.8 0.7 copy-start.9
  21.5 0.7 copy-start.10
  22.2 0.7 copy-start.11
  22.8 8.7 %copy-start.3 = (s32[4,2048]{1,0:T(4,128)S(1)}, s32[4,2048]{1,0:T(4,128)}, u32[]{:S(2)}) copy-start(s32[4,2048]{1,0:T(4,128)} %pairs_x.1) | copy-start | bytes 98308
  22.8 8.7 %copy-start.4 = (s32[4,2048]{1,0:T(4,128)S(1)}, s32[4,2048]{1,0:T(4,128)}, u32[]{:S(2)}) copy-start(s32[4,2048]{1,0:T(4,128)} %pairs_y.1) | copy-start | bytes 98308
  44.7 58.3 %collective-permute-start.6 = (bf16[288,512]{1,0:T(8,128)(2,1)S(1)}, bf16[288,512]{1,0:T(8,128)(2,1)S(1)}, u32[]{:S(2)}, u32[]{:S(2)}) collective-permute-start(bf16[288,512]{1,0:T(8,128)(2,1)S(1)} %get-tuple-element.31), channel_id=1, source_target_pairs={{0,2},{2,4},{4,6},{6,8},{8,10},{10,12},{12,14},{14,16},{16,18},{18... | collective-permute-start | bytes 884744 | tf_op jit(solution)/shard_map/ppermute | solution.py:25
  44.7 58.3 %collective-permute-start.7 = (bf16[288,512]{1,0:T(8,128)(2,1)S(1)}, bf16[288,512]{1,0:T(8,128)(2,1)S(1)}, u32[]{:S(2)}, u32[]{:S(2)}) collective-permute-start(bf16[288,512]{1,0:T(8,128)(2,1)S(1)} %get-tuple-element.32), channel_id=1, source_target_pairs={{0,1},{1,0},{2,3},{3,2},{4,5},{5,4},{6,7},{7,6},{8,9},{9,8},{10,11... | collective-permute-start | bytes 884744 | tf_op jit(solution)/shard_map/ppermute | solution.py:25
